TPU v7x, 32 devices: a whole 2x2x4 slice. The times are simulated.
32 devices in a mesh: fsdp: 8 (over z, x), ctx: 4 (over y, core).
Axes of the slice: x: 2, y: 2, z: 4, core: 2. Of those that a mesh axis runs over, the one named last changes fastest.
Arguments:
- tokens: bfloat16 [16, 592, 1024], P('fsdp', 'ctx'), may hold values from -6 to 6
- out_grad: bfloat16 [16, 592, 1024], P('fsdp', 'ctx'), may hold values from -6 to 6
- key_mask: int32 [16, 592], P('fsdp', 'ctx'), may hold values from 0 to 1, as said below
- slot_valid: int32 [16], P('fsdp'), may hold values 0 or 1
- norm_gains: bfloat16 [2, 1024], P(None, 'fsdp'), may hold values from 0.25 to 1.75
- norm_shifts: bfloat16 [2, 1024], P(None, 'fsdp'), may hold values from -2 to 2
- qkv_weight: bfloat16 [1024, 3072], P('fsdp'), may hold values from -0.1875 to 0.1875
- qv_bias: bfloat16 [2, 1024], P(None, 'fsdp'), may hold values from -3 to 3
- out_weight: bfloat16 [1024, 1024], P('fsdp'), may hold values from -1.5 to 1.5
- out_bias: bfloat16 [1024], P('fsdp'), may hold values from -2 to 2
- fc1_weight: bfloat16 [1024, 4096], P('fsdp'), may hold values from -0.1875 to 0.1875
- fc1_bias: bfloat16 [4096], P('fsdp'), may hold values from -3 to 3
- fc2_weight: bfloat16 [4096, 1024], P('fsdp'), may hold values from -0.125 to 0.125
- fc2_bias: bfloat16 [1024], P('fsdp'), may hold values from -2 to 2
Outputs:
- result: bfloat16 [16, 592, 1024], P('fsdp', 'ctx')
- token_gradient: bfloat16 [16, 592, 1024], P('fsdp', 'ctx')
- gain_grads: float32 [2, 1024], P(None, 'fsdp')
- shift_grads: float32 [2, 1024], P(None, 'fsdp')
- qkv_grad: float32 [1024, 3072], P('fsdp')
- qv_bias_grad: float32 [2, 1024], P(None, 'fsdp')
- out_weight_grad: float32 [1024, 1024], P('fsdp')
- out_bias_grad: float32 [1024], P('fsdp')
- fc1_grad: float32 [1024, 4096], P('fsdp')
- fc1_bias_grad: float32 [4096], P('fsdp')
- fc2_grad: float32 [4096, 1024], P('fsdp')
- fc2_bias_grad: float32 [1024], P('fsdp')
Inputs may be any that keep to these rules, and one draw needn't show every extreme that they name: key_mask is 1 at position 0 of every image and 0 at positions 577 and beyond.
All inputs are finite; a program needn't handle non-finite values. No bound on the sum of `slot_valid` on one device may be relied on, other than what follows from the above.
Results may differ from a plain program's by a relative error of at most 0.017.
Values may be sent and summed in bfloat16 or wider, within the bound.
No kernel may reach another device: no remote copies, remote signals or barrier semaphores. Data moves between devices by JAX's collectives and lax.ppermute only.
A program may use at most 192 MiB of HBM per device.

v0:
```python
import jax
import jax.numpy as jnp
from jax import lax
from jax.sharding import PartitionSpec as P

D = 1024
HEADS = 16
HEAD_DIM = 64
LIVE = 577


def across_rows(left_side, right_side):
    return lax.dot_general(
        left_side, right_side, (((0,), (0,)), ((), ())), preferred_element_type=jnp.float32
    )


def against(left_side, right_side):
    return lax.dot_general(
        left_side, right_side, (((1,), (1,)), ((), ())), preferred_element_type=jnp.float32
    )


def apply_layer_norm(values, gain_row, shift_row):
    centred = values - jnp.mean(values, axis=-1, keepdims=True)
    inverse_std = lax.rsqrt(jnp.mean(centred * centred, axis=-1, keepdims=True) + 1e-05)
    normed = centred * inverse_std
    return (normed * gain_row + shift_row, normed, inverse_std)


def norm_reverse_pass(grad_normed, normed, inverse_std):
    first_mean = jnp.mean(grad_normed, axis=-1, keepdims=True)
    second_mean = jnp.mean(grad_normed * normed, axis=-1, keepdims=True)
    return inverse_std * (grad_normed - first_mean - normed * second_mean)


def head_slice(source, head_index, offset):
    return lax.dynamic_slice_in_dim(source, offset + head_index * HEAD_DIM, HEAD_DIM, 2)


def body(
    tokens,
    out_grad,
    key_mask,
    slot_valid,
    norm_gains,
    norm_shifts,
    qkv_weight,
    qv_bias,
    out_weight,
    out_bias,
    fc1_weight,
    fc1_bias,
    fc2_weight,
    fc2_bias,
):
    full_params = (
        lax.all_gather(norm_gains, "fsdp", axis=1, tiled=True),
        lax.all_gather(norm_shifts, "fsdp", axis=1, tiled=True),
        lax.all_gather(qkv_weight, "fsdp", axis=0, tiled=True),
        lax.all_gather(qv_bias, "fsdp", axis=1, tiled=True),
        lax.all_gather(out_weight, "fsdp", axis=0, tiled=True),
        lax.all_gather(out_bias, "fsdp", axis=0, tiled=True),
        lax.all_gather(fc1_weight, "fsdp", axis=0, tiled=True),
        lax.all_gather(fc1_bias, "fsdp", axis=0, tiled=True),
        lax.all_gather(fc2_weight, "fsdp", axis=0, tiled=True),
        lax.all_gather(fc2_bias, "fsdp", axis=0, tiled=True),
    )
    norm_gain_vector = full_params[0].astype(jnp.float32)
    norm_bias_vector = full_params[1].astype(jnp.float32)
    qkv_matrix = full_params[2]
    qv_shift = full_params[3].astype(jnp.float32)
    out_matrix = full_params[4]
    out_shift = full_params[5].astype(jnp.float32)
    fc1_matrix = full_params[6]
    fc1_shift = full_params[7].astype(jnp.float32)
    fc2_matrix = full_params[8]
    fc2_shift = full_params[9].astype(jnp.float32)
    image_count = tokens.shape[0]
    local_len = tokens.shape[1]
    row_count = image_count * local_len
    flattened_rows = tokens.reshape(row_count, D).astype(jnp.float32)
    normalized_input, first_centred_scaled, first_inverse_deviation = apply_layer_norm(
        flattened_rows, norm_gain_vector[0], norm_bias_vector[0]
    )
    normed_low = normalized_input.astype(jnp.bfloat16)
    raw_proj = jnp.dot(normed_low, qkv_matrix, preferred_element_type=jnp.float32)
    queries = (
        (raw_proj[:, :D] + qv_shift[0]).astype(jnp.bfloat16).reshape(image_count, local_len, D)
    )
    key_value = jnp.concatenate(
        [raw_proj[:, D : 2 * D], raw_proj[:, 2 * D :] + qv_shift[1]], axis=1
    )
    key_value = key_value.astype(jnp.bfloat16).reshape(image_count, local_len, 2 * D)
    key_all, mask_all = (
        lax.all_gather(key_value, "ctx", axis=1, tiled=True),
        lax.all_gather(key_mask.astype(jnp.bfloat16), "ctx", axis=1, tiled=True),
    )
    visible = (mask_all > 0)[:, None, :]

    def head_forward(head_index):
        head_queries = head_slice(queries, head_index, 0)
        head_keys = head_slice(key_all, head_index, 0)
        head_value_rows = head_slice(key_all, head_index, D)
        scores = (
            jnp.einsum("jgz,jaz->jga", head_queries, head_keys, preferred_element_type=jnp.float32)
            * 0.125
        )
        scores = jnp.where(visible, scores, -1e30)
        row_max = jnp.max(scores, axis=-1, keepdims=True)
        exponent = jnp.exp(scores - row_max)
        row_sum = jnp.sum(exponent, axis=-1, keepdims=True)
        attention_weights = (exponent / row_sum).astype(jnp.bfloat16)
        context = jnp.einsum(
            "ans,ash->anh", attention_weights, head_value_rows, preferred_element_type=jnp.float32
        )
        return (context.astype(jnp.bfloat16), (row_max + jnp.log(row_sum))[:, :, 0])

    contexts, log_norm = lax.map(head_forward, jnp.arange(HEADS))
    context_low = contexts.transpose(1, 2, 0, 3).reshape(row_count, D)
    residual_state = (
        flattened_rows
        + jnp.dot(context_low, out_matrix, preferred_element_type=jnp.float32)
        + out_shift
    )
    normalized_residual, second_centred_scaled, second_inverse_deviation = apply_layer_norm(
        residual_state, norm_gain_vector[1], norm_bias_vector[1]
    )
    middle_low = normalized_residual.astype(jnp.bfloat16)
    pre_act = jnp.dot(middle_low, fc1_matrix, preferred_element_type=jnp.float32) + fc1_shift
    sigmoid_gate = jax.nn.sigmoid(1.702 * pre_act)
    hidden = (pre_act * sigmoid_gate).astype(jnp.bfloat16)
    output = (
        residual_state + jnp.dot(hidden, fc2_matrix, preferred_element_type=jnp.float32) + fc2_shift
    )
    result = output.astype(jnp.bfloat16).reshape(image_count, local_len, D)
    position = lax.axis_index("ctx") * local_len + jnp.arange(local_len)
    keep_row = (position < LIVE)[None, :] & (slot_valid[:, None] > 0)
    grad_out = jnp.where(keep_row[:, :, None], out_grad, jnp.zeros_like(out_grad)).reshape(
        row_count, D
    )
    held = lax.optimization_barrier(
        ((norm_gains, qkv_weight, out_weight, fc1_weight, fc2_weight), grad_out)
    )
    held_gain, held_qkv, held_out, held_fc1, held_fc2 = held[0]
    again_params = (
        lax.all_gather(held_gain, "fsdp", axis=1, tiled=True),
        lax.all_gather(held_qkv, "fsdp", axis=0, tiled=True),
        lax.all_gather(held_out, "fsdp", axis=0, tiled=True),
        lax.all_gather(held_fc1, "fsdp", axis=0, tiled=True),
        lax.all_gather(held_fc2, "fsdp", axis=0, tiled=True),
    )
    reverse_gain_pass = again_params[0].astype(jnp.float32)
    back_qkv = again_params[1]
    back_out = again_params[2]
    back_fc1 = again_params[3]
    back_fc2 = again_params[4]
    grad_fc2 = across_rows(hidden, grad_out)
    grad_fc2_shift = jnp.sum(grad_out.astype(jnp.float32), axis=0)
    grad_hidden = against(grad_out, back_fc2)
    grad_pre = grad_hidden * (sigmoid_gate + 1.702 * pre_act * sigmoid_gate * (1.0 - sigmoid_gate))
    grad_fc1_shift = jnp.sum(grad_pre, axis=0)
    grad_pre_low = grad_pre.astype(jnp.bfloat16)
    grad_fc1 = across_rows(middle_low, grad_pre_low)
    middle_norm_gradient = against(grad_pre_low, back_fc1)
    second_gain_gradient = jnp.sum(middle_norm_gradient * second_centred_scaled, axis=0)
    grad_shift_two = jnp.sum(middle_norm_gradient, axis=0)
    residual_gradient = grad_out.astype(jnp.float32) + norm_reverse_pass(
        middle_norm_gradient * reverse_gain_pass[1], second_centred_scaled, second_inverse_deviation
    )
    grad_out_shift = jnp.sum(residual_gradient, axis=0)
    grad_middle_low = residual_gradient.astype(jnp.bfloat16)
    grad_out_matrix = across_rows(context_low, grad_middle_low)
    grad_context = (
        against(grad_middle_low, back_out).astype(jnp.bfloat16).reshape(image_count, local_len, D)
    )

    def head_backward(head_inputs):
        head_index, head_norm = head_inputs
        head_queries = head_slice(queries, head_index, 0)
        head_keys = head_slice(key_all, head_index, 0)
        head_value_rows = head_slice(key_all, head_index, D)
        head_gradient = head_slice(grad_context, head_index, 0)
        scores = (
            jnp.einsum("jgz,jaz->jga", head_queries, head_keys, preferred_element_type=jnp.float32)
            * 0.125
        )
        attention_weights = jnp.where(visible, jnp.exp(scores - head_norm[:, :, None]), 0.0)
        grad_probs = jnp.einsum(
            "jgz,jaz->jga", head_gradient, head_value_rows, preferred_element_type=jnp.float32
        )
        row_delta = jnp.sum(attention_weights * grad_probs, axis=-1, keepdims=True)
        score_gradient = (attention_weights * (grad_probs - row_delta)).astype(jnp.bfloat16)
        grad_query = (
            jnp.einsum(
                "ans,ash->anh", score_gradient, head_keys, preferred_element_type=jnp.float32
            )
            * 0.125
        )
        grad_key = (
            jnp.einsum(
                "isl,isc->ilc", score_gradient, head_queries, preferred_element_type=jnp.float32
            )
            * 0.125
        )
        grad_value = jnp.einsum(
            "isl,isc->ilc",
            attention_weights.astype(jnp.bfloat16),
            head_gradient,
            preferred_element_type=jnp.float32,
        )
        return (grad_query, grad_key, grad_value)

    grad_queries, grad_keys, grad_values = lax.map(head_backward, (jnp.arange(HEADS), log_norm))
    grad_keys_all = grad_keys.transpose(1, 2, 0, 3).reshape(image_count, -1, D)
    grad_values_all = grad_values.transpose(1, 2, 0, 3).reshape(image_count, -1, D)
    own_keys, own_values = (
        lax.psum_scatter(
            grad_keys_all.astype(jnp.bfloat16), "ctx", scatter_dimension=1, tiled=True
        ).astype(jnp.float32),
        lax.psum_scatter(
            grad_values_all.astype(jnp.bfloat16), "ctx", scatter_dimension=1, tiled=True
        ).astype(jnp.float32),
    )
    grad_query_rows = grad_queries.transpose(1, 2, 0, 3).reshape(row_count, D)
    own_value_rows = own_values.reshape(row_count, D)
    grad_qv_shift = jnp.stack([jnp.sum(grad_query_rows, axis=0), jnp.sum(own_value_rows, axis=0)])
    grad_raw = jnp.concatenate(
        [grad_query_rows, own_keys.reshape(row_count, D), own_value_rows], axis=1
    ).astype(jnp.bfloat16)
    grad_qkv = across_rows(normed_low, grad_raw)
    input_norm_gradient = against(grad_raw, back_qkv)
    first_gain_gradient = jnp.sum(input_norm_gradient * first_centred_scaled, axis=0)
    grad_shift_one = jnp.sum(input_norm_gradient, axis=0)
    token_gradient = residual_gradient + norm_reverse_pass(
        input_norm_gradient * reverse_gain_pass[0], first_centred_scaled, first_inverse_deviation
    )
    token_gradient = token_gradient.astype(jnp.bfloat16).reshape(image_count, local_len, D)
    grad_gains = jnp.stack([first_gain_gradient, second_gain_gradient])
    grad_shifts = jnp.stack([grad_shift_one, grad_shift_two])
    (
        gain_part,
        shift_part,
        qkv_part,
        qv_part,
        out_part,
        out_shift_part,
        fc1_part,
        fc1_shift_part,
        fc2_part,
        fc2_shift_part,
    ) = (
        lax.psum_scatter(grad_gains, "fsdp", scatter_dimension=1, tiled=True),
        lax.psum_scatter(grad_shifts, "fsdp", scatter_dimension=1, tiled=True),
        lax.psum_scatter(grad_qkv, "fsdp", scatter_dimension=0, tiled=True),
        lax.psum_scatter(grad_qv_shift, "fsdp", scatter_dimension=1, tiled=True),
        lax.psum_scatter(grad_out_matrix, "fsdp", scatter_dimension=0, tiled=True),
        lax.psum_scatter(grad_out_shift, "fsdp", scatter_dimension=0, tiled=True),
        lax.psum_scatter(grad_fc1, "fsdp", scatter_dimension=0, tiled=True),
        lax.psum_scatter(grad_fc1_shift, "fsdp", scatter_dimension=0, tiled=True),
        lax.psum_scatter(grad_fc2, "fsdp", scatter_dimension=0, tiled=True),
        lax.psum_scatter(grad_fc2_shift, "fsdp", scatter_dimension=0, tiled=True),
    )
    finished = (
        lax.psum(gain_part.astype(jnp.bfloat16), "ctx").astype(jnp.float32),
        lax.psum(shift_part.astype(jnp.bfloat16), "ctx").astype(jnp.float32),
        lax.psum(qkv_part.astype(jnp.bfloat16), "ctx").astype(jnp.float32),
        lax.psum(qv_part.astype(jnp.bfloat16), "ctx").astype(jnp.float32),
        lax.psum(out_part.astype(jnp.bfloat16), "ctx").astype(jnp.float32),
        lax.psum(out_shift_part.astype(jnp.bfloat16), "ctx").astype(jnp.float32),
        lax.psum(fc1_part.astype(jnp.bfloat16), "ctx").astype(jnp.float32),
        lax.psum(fc1_shift_part.astype(jnp.bfloat16), "ctx").astype(jnp.float32),
        lax.psum(fc2_part.astype(jnp.bfloat16), "ctx").astype(jnp.float32),
        lax.psum(fc2_shift_part.astype(jnp.bfloat16), "ctx").astype(jnp.float32),
    )
    return (
        result,
        token_gradient,
        finished[0],
        finished[1],
        finished[2],
        finished[3],
        finished[4],
        finished[5],
        finished[6],
        finished[7],
        finished[8],
        finished[9],
    )


def solution(mesh):
    in_specs = (
        P("fsdp", "ctx", None),
        P("fsdp", "ctx", None),
        P("fsdp", "ctx"),
        P("fsdp"),
        P(None, "fsdp"),
        P(None, "fsdp"),
        P("fsdp", None),
        P(None, "fsdp"),
        P("fsdp", None),
        P("fsdp"),
        P("fsdp", None),
        P("fsdp"),
        P("fsdp", None),
        P("fsdp"),
    )
    out_specs = (
        P("fsdp", "ctx", None),
        P("fsdp", "ctx", None),
        P(None, "fsdp"),
        P(None, "fsdp"),
        P("fsdp", None),
        P(None, "fsdp"),
        P("fsdp", None),
        P("fsdp"),
        P("fsdp", None),
        P("fsdp"),
        P("fsdp", None),
        P("fsdp"),
    )
    return jax.shard_map(body, mesh=mesh, in_specs=in_specs, out_specs=out_specs, check_vma=False)
```

profile of v0, /device:TPU:0, one launch (start us, length us, event | category | flops | bytes accessed | tf_op | source)
XLA Modules:
  0.0 2301.7 jit_solution(17001615898816371938)
XLA Ops:
  13.6 22.3 all_gather.53
  36.0 16.5 all_gather.52
  52.4 18.4 all_gather.55
  70.8 41.2 %all-gather.14.cloned.1.call-done = bf16[1024,3072]{1,0:T(8,128)(2,1)} async-done(((bf16[128,3072]{1,0:T(8,128)(2,1)}), bf16[1024,3072]{1,0:T(8,128)(2,1)}) %all-gather.14.cloned.1.call-update) | async-done | bytes 6291472 | tf_op jit(solution)/shard_map/all_gather | solution.py:60
  112.0 5.0 fusion.46
  127.8 17.6 all-gather.1
  145.4 5.1 all-gather
  150.7 26.1 %all-gather.2 = bf16[8,1,512]{2,1,0:T(2,128)(2,1)S(1)} all-gather(bf16[1,1,512]{2,1,0:T(2,128)(2,1)S(1)} %reshape.215), channel_id=1, replica_groups=mesh['fsdp'=8,'ctx'=4] {'fsdp'}, dimensions={0}, use_global_device_ids=true | all-gather | bytes 9216 | tf_op jit(solution)/shard_map/all_gather | solution.py:65
  176.8 16.7 all_gather.65
  194.2 11.7 copy.101
  205.9 88.4 %while.30 = (s32[]{:T(128)}, bf16[16,2,148,64]{2,3,1,0:T(8,128)(2,1)}, f32[16,2,148]{2,1,0:T(2,128)}, pred[2,1,592]{2,0,1:T(4,128)(4,1)S(1)}, s32[16]{0:T(128)S(...) while((s32[]{:T(128)}, ...), condition=%wide.region_5.6_spmd, body=%wide.region_2.5_spmd.sunk | while | flops 46279904 | bytes 2574702 | solution.py:119
  298.2 2.7 fusion.54
  301.2 35.1 %all-gather.20.cloned.1.call-done = bf16[1024,4096]{1,0:T(8,128)(2,1)} async-done(((bf16[128,4096]{1,0:T(8,128)(2,1)}), bf16[1024,4096]{1,0:T(8,128)(2,1)}) %all-gather.20.cloned.1.call-update) | async-done | bytes 8388624 | tf_op jit(solution)/shard_map/all_gather | solution.py:64
  336.3 8.5 convolution_add_fusion
  344.8 116.7 %all-gather.24.cloned.1.call-done = bf16[4096,1024]{1,0:T(8,128)(2,1)} async-done(((bf16[512,1024]{1,0:T(8,128)(2,1)}), bf16[4096,1024]{1,0:T(8,128)(2,1)}) %all-gather.24.cloned.1.call-update) | async-done | bytes 8388624 | tf_op jit(solution)/shard_map/all_gather | solution.py:151
  461.4 10.3 fusion.55
  471.7 114.9 %all-gather.26.cloned.1.call-done = bf16[1024,4096]{1,0:T(8,128)(2,1)} async-done(((bf16[128,4096]{1,0:T(8,128)(2,1)}), bf16[1024,4096]{1,0:T(8,128)(2,1)}) %all-gather.26.cloned.1.call-update) | async-done | bytes 8388624 | tf_op jit(solution)/shard_map/all_gather | solution.py:150
  586.6 6.5 multiply_reduce_fusion.1
  594.7 41.5 %all-gather.28.cloned.1.call-done = bf16[1024,1024]{1,0:T(8,128)(2,1)} async-done(((bf16[128,1024]{1,0:T(8,128)(2,1)}), bf16[1024,1024]{1,0:T(8,128)(2,1)}) %all-gather.28.cloned.1.call-update) | async-done | bytes 2097168 | tf_op jit(solution)/shard_map/all_gather | solution.py:149
  636.2 3.6 convolution_convert_fusion.1
  644.0 165.1 %while.31 = (s32[]{:T(128)}, f32[16,2,148,64]{2,3,1,0:T(8,128)}, bf16[16,2,592,64]{2,3,1,0:T(8,128)(2,1)}, bf16[16,2,592,64]{2,3,1,0:T(8,128)(2,1)}, pred[2,1,59...) while((s32[]{:T(128)}, f32[16,2,148,64]{2,3,1,0:T(8,128)}, ...), condition=%wide.region_12.13_spmd, body=%wide.region_10.12_spmd.sunk | while | flops 113820000 | bytes 11654198 | solution.py:214
  809.2 3.5 copy.108
  812.7 6.6 copy.109
  819.3 3.5 copy.111
  822.8 6.6 copy.112
  830.4 4.6 fusion.42
  843.6 80.8 %all-reduce.14.cloned.1.call-done = (bf16[2,592,1024]{2,0,1:T(2,128)(2,1)}, bf16[2,592,1024]{2,0,1:T(2,128)(2,1)}) async-done(((bf16[2,592,1024]{2,0,1:T(2,128)(2,1)}, bf16[2,592,1024]{2,0,1:T(2,128)(2,1)}), (bf16[2,592,1024]{2,0,1:T(2,128)(2,1)}, bf16[2,592,1024]{2,0,1:T(2,128)(2,1)})) %all-reduce.14.cloned.1.call-update) | async-done | bytes 4849680
  933.9 8.3 fusion.45
  942.2 10.3 fusion.38
  953.6 10.7 fusion.47
  966.9 58.9 %all-gather.30.cloned.1.call-done = bf16[1024,3072]{1,0:T(8,128)(2,1)} async-done(((bf16[128,3072]{1,0:T(8,128)(2,1)}), bf16[1024,3072]{1,0:T(8,128)(2,1)}) %all-gather.30.cloned.1.call-update) | async-done | bytes 6291472 | tf_op jit(solution)/shard_map/all_gather | solution.py:148
  1025.8 6.7 multiply_reduce_fusion.2
  1035.8 18.2 all-gather.3
  1056.0 59.5 %reduce-scatter.16.cloned.1.call-done = f32[128,1024]{1,0:T(8,128)} async-done(((f32[1024,1024]{1,0:T(8,128)}), f32[128,1024]{1,0:T(8,128)}) %reduce-scatter.16.cloned.1.call-update) | async-done | bytes 524304 | tf_op jit(solution)/shard_map/reduce_scatter | solution.py:257
  1117.2 209.3 %reduce-scatter.14.cloned.1.call-done = f32[128,3072]{1,0:T(8,128)} async-done(((f32[1024,3072]{1,0:T(8,128)}), f32[128,3072]{1,0:T(8,128)}) %reduce-scatter.14.cloned.1.call-update) | async-done | bytes 1572880 | tf_op jit(solution)/shard_map/reduce_scatter | solution.py:255
  1328.9 283.5 %reduce-scatter.18.cloned.1.call-done = f32[128,4096]{1,0:T(8,128)} async-done(((f32[1024,4096]{1,0:T(8,128)}), f32[128,4096]{1,0:T(8,128)}) %reduce-scatter.18.cloned.1.call-update) | async-done | bytes 2097168 | tf_op jit(solution)/shard_map/reduce_scatter | solution.py:259
  1612.4 2.7 convert_element_type.217
  1615.1 282.9 %reduce-scatter.20.cloned.1.call-done = f32[512,1024]{1,0:T(8,128)} async-done(((f32[4096,1024]{1,0:T(8,128)}), f32[512,1024]{1,0:T(8,128)}) %reduce-scatter.20.cloned.1.call-update) | async-done | bytes 2097168 | tf_op jit(solution)/shard_map/reduce_scatter | solution.py:261
  1898.0 2.8 convert_element_type.221
  1900.8 123.4 %all-gather.22.cloned.1.call-done = bf16[4096,1024]{1,0:T(8,128)(2,1)} async-done(((bf16[512,1024]{1,0:T(8,128)(2,1)}), bf16[4096,1024]{1,0:T(8,128)(2,1)}) %all-gather.22.cloned.1.call-update) | async-done | bytes 8388624 | tf_op jit(solution)/shard_map/all_gather | solution.py:66
  2024.2 8.5 fusion.35
  2035.5 34.2 %all-reduce.5 = (bf16[1024]{0:T(1024)(128)(2,1)S(1)}, bf16[4096]{0:T(1024)(128)(2,1)S(1)}, bf16[1024]{0:T(1024)(128)(2,1)S(1)}) all-reduce(f32[1024]{0:T(1024)S(1)} %get-tuple-element.448, f32[4096]{0:T(1024)S(1)} %get-tuple-element.470, f32[1024]{0:T(1024)S(1)} %get-tuple-element.446), channel_id=9, replica_groups=mesh['fsdp'=8,'ctx'=4] {'fsdp'}, use_global_device_ids=true, to_apply=%region_34.35.clone | all-reduce | flops 6144 | bytes 36864
  2073.2 15.2 reduce-scatter.22.cloned.1.call-done
  2089.3 63.3 %reduce-scatter.24.cloned.1.call-done = f32[128,2]{1,0:T(8,128)} async-done(((f32[1024,2]{1,0:T(8,128)}), f32[128,2]{1,0:T(8,128)}) %reduce-scatter.24.cloned.1.call-update) | async-done | bytes 1040
  2153.5 63.5 %reduce-scatter.26.cloned.1.call-done = f32[128,2]{1,0:T(8,128)} async-done(((f32[1024,2]{1,0:T(8,128)}), f32[128,2]{1,0:T(8,128)}) %reduce-scatter.26.cloned.1.call-update) | async-done | bytes 1040
  2218.0 5.7 all-reduce.6
  2226.9 61.3 %all-reduce.12.cloned.1.call-done = (bf16[128,3072]{1,0:T(8,128)(2,1)}, bf16[128,1024]{1,0:T(8,128)(2,1)}, bf16[128,4096]{1,0:T(8,128)(2,1)}, bf16[512,1024]{1,0:T(8,128)(2,1)}) async-done(((bf16[128,3072]{1,0:T(8,128)(2,1)}, bf16[128,1024]{1,0:T(8,128)(2,1)}, bf16[128,4096]{1,0:T(8,128)(2,1)}, bf16[512,1024]{1,0:T(8,128)(2,1)}), (bf16[128,3072]{1,0:T(8,128)(2,1)}, bf16[128,1024]{1,0:T(8,128)(2,1)}, ...) | async-done | bytes 3145744 | tf_op jit(solution)/shard_map/psum | solution.py:267
  2288.2 2.5 convert_element_type.209
  (448 shorter events, 305.6 us)
Async XLA Ops:
  7.2 104.9 %all-gather.14.cloned.1.call-start = ((), (), s32[]{:S(2)}) async-start(), calls=%async_computation.7 | async-start | bytes 7077888 | tf_op jit(solution)/shard_map/all_gather | solution.py:60
  7.9 3.9 copy-start.1
  7.9 186.2 %all-gather.16.cloned.1.call-start = ((), (), s32[]{:S(2)}) async-start(), calls=%async_computation.8 | async-start | bytes 6062080 | tf_op jit(solution)/shard_map/all_gather | solution.py:96
  10.3 3.3 copy-start.15
  10.3 25.7 %copy-start.12 = (bf16[2,128]{1,0:T(2,128)(2,1)S(1)}, bf16[2,128]{1,0:T(2,128)(2,1)}, u32[]{:S(2)}) copy-start(bf16[2,128]{1,0:T(2,128)(2,1)} %param.22) | copy-start | bytes 1540
  10.3 42.1 %copy-start.16 = (bf16[2,128]{1,0:T(2,128)(2,1)S(1)}, bf16[2,128]{1,0:T(2,128)(2,1)}, u32[]{:S(2)}) copy-start(bf16[2,128]{1,0:T(2,128)(2,1)} %param.25) | copy-start | bytes 1540
  122.8 175.4 %all-gather.18.cloned.1.call-start = ((), (), s32[]{:S(2)}) async-start(), calls=%async_computation.9 | async-start | bytes 2359296 | tf_op jit(solution)/shard_map/all_gather | solution.py:62
  123.5 212.7 %all-gather.20.cloned.1.call-start = ((), (), s32[]{:S(2)}) async-start(), calls=%async_computation.10 | async-start | bytes 9437184 | tf_op jit(solution)/shard_map/all_gather | solution.py:64
  124.1 337.3 %all-gather.24.cloned.1.call-start = ((), (), s32[]{:S(2)}) async-start(), calls=%async_computation.12 | async-start | bytes 9437184 | tf_op jit(solution)/shard_map/all_gather | solution.py:151
  125.4 2.4 copy-start.17
  125.4 20.1 copy-start.13
  125.4 25.3 %copy-start.14 = (bf16[512]{0:T(512)(128)(2,1)S(1)}, bf16[512]{0:T(512)(128)(2,1)}, u32[]{:S(2)}) copy-start(bf16[512]{0:T(512)(128)(2,1)} %param.29) | copy-start | bytes 3076
  125.4 68.1 %copy-start.5 = (bf16[296,1024]{1,0:T(8,128)(2,1)S(1)}, bf16[296,1024]{1,0:T(8,128)(2,1)}, u32[]{:S(2)}) copy-start(bf16[296,1024]{1,0:T(8,128)(2,1)} %get-tuple-element.457) | copy-start | bytes 1818628
  126.4 460.2 %all-gather.26.cloned.1.call-start = ((), (), s32[]{:S(2)}) async-start(), calls=%async_computation.13 | async-start | bytes 9437184 | tf_op jit(solution)/shard_map/all_gather | solution.py:150
  127.0 509.2 %all-gather.28.cloned.1.call-start = ((), (), s32[]{:S(2)}) async-start(), calls=%async_computation.14 | async-start | bytes 2359296 | tf_op jit(solution)/shard_map/all_gather | solution.py:149
  127.7 796.7 %all-reduce.14.cloned.1.call-start = ((), (), s32[]{:S(2)}) async-start(), calls=%async_computation.24 | async-start | bytes 9699328
  586.6 6.6 copy-start.6
  649.0 5.4 copy-start.3
  659.3 5.4 copy-start.3
  669.6 5.4 copy-start.3
  679.9 5.4 copy-start.3
  690.2 5.4 copy-start.3
  700.6 5.4 copy-start.3
  710.9 5.4 copy-start.3
  721.2 5.4 copy-start.3
  731.5 5.4 copy-start.3
  741.8 5.4 copy-start.3
  752.1 5.4 copy-start.3
  762.4 5.4 copy-start.3
  772.8 5.4 copy-start.3
  783.1 5.4 copy-start.3
  793.4 5.4 copy-start.3
  803.8 5.4 copy-start.3
  829.4 196.4 %all-gather.30.cloned.1.call-start = ((), (), s32[]{:S(2)}) async-start(), calls=%async_computation.15 | async-start | bytes 7077888 | tf_op jit(solution)/shard_map/all_gather | solution.py:148
  830.1 285.3 %reduce-scatter.16.cloned.1.call-start = ((), (), s32[]{:S(2)}) async-start(), calls=%async_computation.17 | async-start | bytes 4718592 | tf_op jit(solution)/shard_map/reduce_scatter | solution.py:257
  835.0 491.5 %reduce-scatter.14.cloned.1.call-start = ((), (), s32[]{:S(2)}) async-start(), calls=%async_computation.16 | async-start | bytes 14155776 | tf_op jit(solution)/shard_map/reduce_scatter | solution.py:255
  942.2 670.2 %reduce-scatter.18.cloned.1.call-start = ((), (), s32[]{:S(2)}) async-start(), calls=%async_computation.18 | async-start | bytes 18874368 | tf_op jit(solution)/shard_map/reduce_scatter | solution.py:259
  952.6 945.4 %reduce-scatter.20.cloned.1.call-start = ((), (), s32[]{:S(2)}) async-start(), calls=%async_computation.19 | async-start | bytes 18874368 | tf_op jit(solution)/shard_map/reduce_scatter | solution.py:261
  964.4 1059.8 %all-gather.22.cloned.1.call-start = ((), (), s32[]{:S(2)}) async-start(), calls=%async_computation.11 | async-start | bytes 9437184 | tf_op jit(solution)/shard_map/all_gather | solution.py:66
  965.0 1123.5 %reduce-scatter.22.cloned.1.call-start = ((), (), s32[]{:S(2)}) async-start(), calls=%async_computation.20 | async-start | bytes 589824
  1032.5 3.4 copy-start.18
  1032.5 21.6 copy-start.20
  1033.5 1119.1 %reduce-scatter.24.cloned.1.call-start = ((), (), s32[]{:S(2)}) async-start(), calls=%async_computation.21 | async-start | bytes 589824
  1034.7 1182.4 %reduce-scatter.26.cloned.1.call-start = ((), (), s32[]{:S(2)}) async-start(), calls=%async_computation.22 | async-start | bytes 589824
  1035.8 1252.4 %all-reduce.12.cloned.1.call-start = ((), (), s32[]{:S(2)}) async-start(), calls=%async_computation.23 | async-start | bytes 6291456 | tf_op jit(solution)/shard_map/psum | solution.py:267
  2032.7 37.2 %copy-start = (f32[296,1024]{1,0:T(8,128)S(1)}, f32[296,1024]{1,0:T(8,128)}, u32[]{:S(2)}) copy-start(f32[296,1024]{1,0:T(8,128)} %get-tuple-element.449) | copy-start | bytes 3637252
  2288.2 2.5 copy-start.11
  2288.2 3.4 copy-start.9
  (22 other events, 29.4 us)
Sparse Core Ops, SparseCore 0:
  10.2 101.8 all-gather.13
  122.9 36.4 all-gather.15
  161.5 49.2 all-gather.17
  212.8 123.4 all-gather.19
  338.3 123.1 all-gather.23
  463.4 123.1 all-gather.25
  588.7 47.4 all-gather.27
  829.5 94.8 all-reduce.13
  926.6 99.1 all-gather.29
  1029.3 86.1 reduce-scatter.15
  1119.4 207.0 reduce-scatter.13
  1330.6 281.7 reduce-scatter.17
  1616.2 281.7 reduce-scatter.19
  1900.2 123.9 all-gather.21
  2028.3 60.0 reduce-scatter.21
  2091.6 60.9 reduce-scatter.23
  2156.2 60.8 reduce-scatter.25
  2220.1 68.0 all-reduce.11
where the time goes:
time: 2310 us; the launch traced here: 2300 us
  waiting for transfers between devices  1660 us (72%)
  matrix products  269 us (12%)
  blocking collectives  181 us (8%)
  local copies, waits for them, and re-layouts  108 us (5%)
  other arithmetic  49 us (2%)
    reduce_scatter x1, waiting for transfers between devices, body(): lax.psum_scatter(grad_fc1, 'fsdp', scatter_dimension=0, tiled=True)  284 us
    reduce_scatter x1, waiting for transfers between devices, body(): lax.psum_scatter(grad_fc2, 'fsdp', scatter_dimension=0, tiled=True)  283 us
    unnamed x22, waiting for transfers between devices  227 us
    reduce_scatter x1, waiting for transfers between devices, body(): lax.psum_scatter(grad_qkv, 'fsdp', scatter_dimension=0, tiled=True)  209 us
    all_gather x1, waiting for transfers between devices, body(): lax.all_gather(fc2_weight, 'fsdp', axis=0, tiled=True)  123 us
    all_gather x1, waiting for transfers between devices, body(): lax.all_gather(held_fc2, 'fsdp', axis=0, tiled=True)  117 us
    all_gather x1, waiting for transfers between devices, body(): lax.all_gather(held_fc1, 'fsdp', axis=0, tiled=True)  115 us
    psum x1, waiting for transfers between devices, body(): lax.psum(qkv_part.astype(jnp.bfloat16), 'ctx').astype(jnp.float32)  61.3 us
  transfers between devices with their start and end apart: 18, of which 16 were waited for; matrix products, arithmetic and copies ran while one was open for 10% of the time, Pallas kernels for 0%

commit v1 on v0

--- a/solution.py
+++ b/solution.py
@@ -2,11 +2,16 @@
 import jax.numpy as jnp
 from jax import lax
 from jax.sharding import PartitionSpec as P
+from jax.lax import all_gather
 
 D = 1024
 HEADS = 16
 HEAD_DIM = 64
 LIVE = 577
+
+
+def carry_the_vector(my_tile, along_axis):
+    return all_gather(my_tile, along_axis).sum(axis=0)
 
 
 def across_rows(left_side, right_side):
@@ -264,7 +269,7 @@
     finished = (
         lax.psum(gain_part.astype(jnp.bfloat16), "ctx").astype(jnp.float32),
         lax.psum(shift_part.astype(jnp.bfloat16), "ctx").astype(jnp.float32),
-        lax.psum(qkv_part.astype(jnp.bfloat16), "ctx").astype(jnp.float32),
+        carry_the_vector(qkv_part.astype(jnp.bfloat16), "ctx").astype(jnp.float32),
         lax.psum(qv_part.astype(jnp.bfloat16), "ctx").astype(jnp.float32),
         lax.psum(out_part.astype(jnp.bfloat16), "ctx").astype(jnp.float32),
         lax.psum(out_shift_part.astype(jnp.bfloat16), "ctx").astype(jnp.float32),

time: 2310 us -> 2120 us (0.918)
  waiting for transfers between devices: 1660 us -> 1460 us
    reduce_scatter x1, waiting for transfers between devices: 284 us -> 181 us  [body(): lax.psum_scatter(grad_fc1, 'fsdp', scatter_dimension=0, tiled=True)]
    unnamed x22, waiting for transfers between devices: 227 us -> 304 us
    psum x1 -> x0, waiting for transfers between devices: 61.3 us -> none  [body(): lax.psum(qkv_part.astype(jnp.bfloat16), 'ctx').astype(jnp.float32)]
    reduce_scatter x1, waiting for transfers between devices: 59.5 us -> 0.01 us  [body(): lax.psum_scatter(grad_out_matrix, 'fsdp', scatter_dimension=0, tiled=True)]
    all_gather x1, waiting for transfers between devices: 123 us -> 69.6 us  [body(): lax.all_gather(fc2_weight, 'fsdp', axis=0, tiled=True)]
    all_gather x1, waiting for transfers between devices: 41.5 us -> 15 us  [body(): lax.all_gather(held_out, 'fsdp', axis=0, tiled=True)]
  transfers between devices with their start and end apart: 18 -> 18, of which waited for: 16 -> 15; matrix products, arithmetic and copies ran while one was open for 10% -> 19% of each run, Pallas kernels for 0% -> 0%
where the time goes in v1:
time: 2120 us; the launch traced here: 2110 us
  waiting for transfers between devices  1460 us (69%)
  matrix products  270 us (13%)
  blocking collectives  181 us (9%)
  local copies, waits for them, and re-layouts  107 us (5%)
  other arithmetic  48 us (2%)
  loops' own time  22.1 us (1%)
    unnamed x22, waiting for transfers between devices  304 us
    reduce_scatter x1, waiting for transfers between devices, body(): lax.psum_scatter(grad_fc2, 'fsdp', scatter_dimension=0, tiled=True)  283 us
    reduce_scatter x1, waiting for transfers between devices, body(): lax.psum_scatter(grad_qkv, 'fsdp', scatter_dimension=0, tiled=True)  201 us
    reduce_scatter x1, waiting for transfers between devices, body(): lax.psum_scatter(grad_fc1, 'fsdp', scatter_dimension=0, tiled=True)  181 us
    all_gather x1, waiting for transfers between devices, body(): lax.all_gather(held_fc2, 'fsdp', axis=0, tiled=True)  117 us
    all_gather x1, waiting for transfers between devices, body(): lax.all_gather(held_fc1, 'fsdp', axis=0, tiled=True)  115 us
    all_gather x1, waiting for transfers between devices, body(): lax.all_gather(held_qkv, 'fsdp', axis=0, tiled=True)  80 us
    all_gather x1, waiting for transfers between devices, body(): lax.all_gather(fc2_weight, 'fsdp', axis=0, tiled=True)  69.6 us
  transfers between devices with their start and end apart: 18, of which 15 were waited for; matrix products, arithmetic and copies ran while one was open for 19% of the time, Pallas kernels for 0%

profile of v1, /device:TPU:0, one launch (start us, length us, event | category | flops | bytes accessed | tf_op | source)
XLA Modules:
  0.0 2107.1 jit_solution(14461050748864809415)
XLA Ops:
  13.6 22.3 %all_gather.58 = bf16[2,1024]{1,0:T(2,128)(2,1)S(1)} all-gather(bf16[2,128]{1,0:T(2,128)(2,1)S(1)} %copy-done.13), channel_id=1, replica_groups=mesh['fsdp'=8,'ctx'=4] {'fsdp'}, dimensions={1}, use_global_device_ids=true | all-gather | bytes 4608 | tf_op jit(solution)/shard_map/all_gather | solution.py:63
  36.0 16.5 all_gather.59
  52.4 18.4 all_gather.61
  70.8 41.2 %all-gather.16.cloned.1.call-done = bf16[1024,3072]{1,0:T(8,128)(2,1)} async-done(((bf16[128,3072]{1,0:T(8,128)(2,1)}), bf16[1024,3072]{1,0:T(8,128)(2,1)}) %all-gather.16.cloned.1.call-update) | async-done | bytes 6291472 | tf_op jit(solution)/shard_map/all_gather | solution.py:65
  112.0 5.0 fusion.46
  127.8 5.1 all-gather.1
  133.0 17.6 all-gather.2
  150.6 26.1 %all-gather.3 = bf16[8,1,512]{2,1,0:T(2,128)(2,1)S(1)} all-gather(bf16[1,1,512]{2,1,0:T(2,128)(2,1)S(1)} %reshape.216), channel_id=1, replica_groups=mesh['fsdp'=8,'ctx'=4] {'fsdp'}, dimensions={0}, use_global_device_ids=true | all-gather | bytes 9216 | tf_op jit(solution)/shard_map/all_gather | solution.py:70
  176.7 16.7 all_gather.71
  194.2 11.7 copy.101
  205.8 88.4 %while.30 = (s32[]{:T(128)}, bf16[16,2,148,64]{2,3,1,0:T(8,128)(2,1)}, f32[16,2,148]{2,1,0:T(2,128)}, pred[2,1,592]{2,0,1:T(4,128)(4,1)S(1)}, s32[16]{0:T(128)S(...) while((s32[]{:T(128)}, ...), condition=%wide.region_5.6_spmd, body=%wide.region_2.5_spmd.sunk | while | flops 46279904 | bytes 2575710 | solution.py:124
  298.2 2.7 fusion.54
  301.2 35.2 %all-gather.22.cloned.1.call-done = bf16[1024,4096]{1,0:T(8,128)(2,1)} async-done(((bf16[128,4096]{1,0:T(8,128)(2,1)}), bf16[1024,4096]{1,0:T(8,128)(2,1)}) %all-gather.22.cloned.1.call-update) | async-done | bytes 8388624 | tf_op jit(solution)/shard_map/all_gather | solution.py:69
  336.3 8.5 convolution_add_fusion
  344.8 116.7 %all-gather.26.cloned.1.call-done = bf16[4096,1024]{1,0:T(8,128)(2,1)} async-done(((bf16[512,1024]{1,0:T(8,128)(2,1)}), bf16[4096,1024]{1,0:T(8,128)(2,1)}) %all-gather.26.cloned.1.call-update) | async-done | bytes 8388624 | tf_op jit(solution)/shard_map/all_gather | solution.py:156
  461.5 10.3 fusion.55
  471.7 114.9 %all-gather.28.cloned.1.call-done = bf16[1024,4096]{1,0:T(8,128)(2,1)} async-done(((bf16[128,4096]{1,0:T(8,128)(2,1)}), bf16[1024,4096]{1,0:T(8,128)(2,1)}) %all-gather.28.cloned.1.call-update) | async-done | bytes 8388624 | tf_op jit(solution)/shard_map/all_gather | solution.py:155
  586.6 6.6 multiply_reduce_fusion.1
  594.7 3.4 fusion.42
  598.2 10.0 fusion.38
  608.3 13.0 fusion.47
  621.3 15.0 all-gather.30.cloned.1.call-done
  636.4 3.6 convolution_convert_fusion.1
  644.2 165.5 %while.31 = (s32[]{:T(128)}, f32[16,2,148,64]{2,3,1,0:T(8,128)}, bf16[16,2,592,64]{2,3,1,0:T(8,128)(2,1)}, bf16[16,2,592,64]{2,3,1,0:T(8,128)(2,1)}, pred[2,1,59...) while((s32[]{:T(128)}, f32[16,2,148,64]{2,3,1,0:T(8,128)}, ...), condition=%wide.region_12.13_spmd, body=%wide.region_10.12_spmd.sunk | while | flops 113820000 | bytes 11655714 | solution.py:219
  809.7 3.7 copy.108
  813.3 6.6 copy.109
  819.9 3.5 copy.111
  823.4 6.7 copy.112
  831.9 181.3 %reduce-scatter.18.cloned.1.call-done = f32[128,4096]{1,0:T(8,128)} async-done(((f32[1024,4096]{1,0:T(8,128)}), f32[128,4096]{1,0:T(8,128)}) %reduce-scatter.18.cloned.1.call-update) | async-done | bytes 2097168 | tf_op jit(solution)/shard_map/reduce_scatter | solution.py:264
  1013.2 2.7 convert_element_type.219
  1015.9 282.8 %reduce-scatter.20.cloned.1.call-done = f32[512,1024]{1,0:T(8,128)} async-done(((f32[4096,1024]{1,0:T(8,128)}), f32[512,1024]{1,0:T(8,128)}) %reduce-scatter.20.cloned.1.call-update) | async-done | bytes 2097168 | tf_op jit(solution)/shard_map/reduce_scatter | solution.py:266
  1298.7 2.7 convert_element_type.223
  1310.3 126.2 %all-reduce.10.cloned.1.call-done = (bf16[2,592,1024]{2,0,1:T(2,128)(2,1)}, bf16[2,592,1024]{2,0,1:T(2,128)(2,1)}, bf16[128,1024]{1,0:T(8,128)(2,1)}, bf16[128,4096]{1,0:T(8,128)(2,1)}, bf16[512,1024]{1,0:T(8,128)(2,1)}) async-done(((bf16[2,592,1024]{2,0,1:T(2,128)(2,1)}, bf16[2,592,1024]{2,0,1:T(2,128)(2,1)}, bf16[128,1024]{1,0:T(8,128)(2,1)}, bf16[128,4096]{1,0:T(8,128)(2,1)}, ...) | async-done | bytes 7208976
  1446.0 8.4 fusion.45
  1458.0 80.0 %all-gather.32.cloned.1.call-done = bf16[1024,3072]{1,0:T(8,128)(2,1)} async-done(((bf16[128,3072]{1,0:T(8,128)(2,1)}), bf16[1024,3072]{1,0:T(8,128)(2,1)}) %all-gather.32.cloned.1.call-update) | async-done | bytes 6291472 | tf_op jit(solution)/shard_map/all_gather | solution.py:153
  1538.0 6.7 multiply_reduce_fusion.2
  1547.0 200.7 %reduce-scatter.14.cloned.1.call-done = f32[128,3072]{1,0:T(8,128)} async-done(((f32[1024,3072]{1,0:T(8,128)}), f32[128,3072]{1,0:T(8,128)}) %reduce-scatter.14.cloned.1.call-update) | async-done | bytes 1572880 | tf_op jit(solution)/shard_map/reduce_scatter | solution.py:260
  1747.6 2.4 convert_element_type.210
  1752.0 18.5 all-gather.4
  1770.5 34.3 %all-reduce.5 = (bf16[1024]{0:T(1024)(128)(2,1)S(1)}, bf16[4096]{0:T(1024)(128)(2,1)S(1)}, bf16[1024]{0:T(1024)(128)(2,1)S(1)}) all-reduce(f32[1024]{0:T(1024)S(1)} %get-tuple-element.447, f32[4096]{0:T(1024)S(1)} %get-tuple-element.469, f32[1024]{0:T(1024)S(1)} %get-tuple-element.445), channel_id=10, replica_groups=mesh['fsdp'=8,'ctx'=4] {'fsdp'}, use_global_device_ids=true, to_apply=%region_34.35.clone | all-reduce | flops 6144 | bytes 36864
  1805.0 69.6 %all-gather.24.cloned.1.call-done = bf16[4096,1024]{1,0:T(8,128)(2,1)} async-done(((bf16[512,1024]{1,0:T(8,128)(2,1)}), bf16[4096,1024]{1,0:T(8,128)(2,1)}) %all-gather.24.cloned.1.call-update) | async-done | bytes 8388624 | tf_op jit(solution)/shard_map/all_gather | solution.py:71
  1874.6 8.5 fusion.35
  1891.9 46.4 %reduce-scatter.26.cloned.1.call-done = f32[128,2]{1,0:T(8,128)} async-done(((f32[1024,2]{1,0:T(8,128)}), f32[128,2]{1,0:T(8,128)}) %reduce-scatter.26.cloned.1.call-update) | async-done | bytes 1040
  1939.3 63.3 %reduce-scatter.24.cloned.1.call-done = f32[128,2]{1,0:T(8,128)} async-done(((f32[1024,2]{1,0:T(8,128)}), f32[128,2]{1,0:T(8,128)}) %reduce-scatter.24.cloned.1.call-update) | async-done | bytes 1040
  2003.5 63.6 %reduce-scatter.22.cloned.1.call-done = f32[128,2]{1,0:T(8,128)} async-done(((f32[1024,2]{1,0:T(8,128)}), f32[128,2]{1,0:T(8,128)}) %reduce-scatter.22.cloned.1.call-update) | async-done | bytes 1040
  2068.1 5.7 all-reduce.6
  2077.0 19.1 all-gather.34.cloned.1.call-done
  2096.2 2.5 reduce_sum.201
  (451 shorter events, 301.8 us)
Async XLA Ops:
  7.2 104.9 %all-gather.16.cloned.1.call-start = ((), (), s32[]{:S(2)}) async-start(), calls=%async_computation.7 | async-start | bytes 7077888 | tf_op jit(solution)/shard_map/all_gather | solution.py:65
  7.9 3.9 copy-start.2
  7.9 186.2 %all-gather.18.cloned.1.call-start = ((), (), s32[]{:S(2)}) async-start(), calls=%async_computation.8 | async-start | bytes 6062080 | tf_op jit(solution)/shard_map/all_gather | solution.py:101
  10.3 3.3 copy-start.13
  10.3 25.7 %copy-start.16 = (bf16[2,128]{1,0:T(2,128)(2,1)S(1)}, bf16[2,128]{1,0:T(2,128)(2,1)}, u32[]{:S(2)}) copy-start(bf16[2,128]{1,0:T(2,128)(2,1)} %param.23) | copy-start | bytes 1540
  10.3 42.1 %copy-start.17 = (bf16[2,128]{1,0:T(2,128)(2,1)S(1)}, bf16[2,128]{1,0:T(2,128)(2,1)}, u32[]{:S(2)}) copy-start(bf16[2,128]{1,0:T(2,128)(2,1)} %param.25) | copy-start | bytes 1540
  122.8 175.3 %all-gather.20.cloned.1.call-start = ((), (), s32[]{:S(2)}) async-start(), calls=%async_computation.9 | async-start | bytes 2359296 | tf_op jit(solution)/shard_map/all_gather | solution.py:67
  123.6 212.8 %all-gather.22.cloned.1.call-start = ((), (), s32[]{:S(2)}) async-start(), calls=%async_computation.10 | async-start | bytes 9437184 | tf_op jit(solution)/shard_map/all_gather | solution.py:69
  124.1 337.3 %all-gather.26.cloned.1.call-start = ((), (), s32[]{:S(2)}) async-start(), calls=%async_computation.12 | async-start | bytes 9437184 | tf_op jit(solution)/shard_map/all_gather | solution.py:156
  125.4 2.4 copy-start.14
  125.4 7.6 copy-start.18
  125.4 25.2 %copy-start.15 = (bf16[512]{0:T(512)(128)(2,1)S(1)}, bf16[512]{0:T(512)(128)(2,1)}, u32[]{:S(2)}) copy-start(bf16[512]{0:T(512)(128)(2,1)} %param.29) | copy-start | bytes 3076
  125.4 68.1 %copy-start.6 = (bf16[296,1024]{1,0:T(8,128)(2,1)S(1)}, bf16[296,1024]{1,0:T(8,128)(2,1)}, u32[]{:S(2)}) copy-start(bf16[296,1024]{1,0:T(8,128)(2,1)} %get-tuple-element.456) | copy-start | bytes 1818628
  126.4 460.2 %all-gather.28.cloned.1.call-start = ((), (), s32[]{:S(2)}) async-start(), calls=%async_computation.13 | async-start | bytes 9437184 | tf_op jit(solution)/shard_map/all_gather | solution.py:155
  127.0 509.4 %all-gather.30.cloned.1.call-start = ((), (), s32[]{:S(2)}) async-start(), calls=%async_computation.14 | async-start | bytes 2359296 | tf_op jit(solution)/shard_map/all_gather | solution.py:154
  127.7 702.4 %reduce-scatter.16.cloned.1.call-start = ((), (), s32[]{:S(2)}) async-start(), calls=%async_computation.17 | async-start | bytes 4718592 | tf_op jit(solution)/shard_map/reduce_scatter | solution.py:262
  586.6 6.6 copy-start.7
  598.1 415.1 %reduce-scatter.18.cloned.1.call-start = ((), (), s32[]{:S(2)}) async-start(), calls=%async_computation.18 | async-start | bytes 18874368 | tf_op jit(solution)/shard_map/reduce_scatter | solution.py:264
  608.2 690.5 %reduce-scatter.20.cloned.1.call-start = ((), (), s32[]{:S(2)}) async-start(), calls=%async_computation.19 | async-start | bytes 18874368 | tf_op jit(solution)/shard_map/reduce_scatter | solution.py:266
  621.3 815.2 %all-reduce.10.cloned.1.call-start = ((), (), s32[]{:S(2)}) async-start(), calls=%async_computation.24 | async-start | bytes 14417920
  649.2 5.4 copy-start.4
  659.5 5.4 copy-start.4
  669.9 5.4 copy-start.4
  680.2 5.4 copy-start.4
  690.5 5.4 copy-start.4
  700.9 5.4 copy-start.4
  711.2 5.4 copy-start.4
  721.5 5.4 copy-start.4
  731.9 5.4 copy-start.4
  742.2 5.4 copy-start.4
  752.5 5.4 copy-start.4
  762.9 5.4 copy-start.4
  773.2 5.4 copy-start.4
  783.6 5.4 copy-start.4
  793.9 5.4 copy-start.4
  804.2 5.4 copy-start.4
  1301.5 236.6 %all-gather.32.cloned.1.call-start = ((), (), s32[]{:S(2)}) async-start(), calls=%async_computation.15 | async-start | bytes 7077888 | tf_op jit(solution)/shard_map/all_gather | solution.py:153
  1302.0 445.6 %reduce-scatter.14.cloned.1.call-start = ((), (), s32[]{:S(2)}) async-start(), calls=%async_computation.16 | async-start | bytes 14155776 | tf_op jit(solution)/shard_map/reduce_scatter | solution.py:260
  1454.3 420.3 %all-gather.24.cloned.1.call-start = ((), (), s32[]{:S(2)}) async-start(), calls=%async_computation.11 | async-start | bytes 9437184 | tf_op jit(solution)/shard_map/all_gather | solution.py:71
  1454.9 483.5 %reduce-scatter.26.cloned.1.call-start = ((), (), s32[]{:S(2)}) async-start(), calls=%async_computation.23 | async-start | bytes 589824
  1458.0 544.6 %reduce-scatter.24.cloned.1.call-start = ((), (), s32[]{:S(2)}) async-start(), calls=%async_computation.22 | async-start | bytes 589824
  1545.8 521.4 %reduce-scatter.22.cloned.1.call-start = ((), (), s32[]{:S(2)}) async-start(), calls=%async_computation.21 | async-start | bytes 589824
  1546.9 203.2 %copy-start.21 = (u32[32]{0:T(128)S(1)}, u32[32]{0:T(128)}, u32[]{:S(2)}) copy-start(u32[32]{0:T(128)} %constant.164) | copy-start | bytes 388
  1546.9 205.1 %copy-start.19 = (bf16[128]{0:T(256)(128)(2,1)S(1)}, bf16[128]{0:T(256)(128)(2,1)}, u32[]{:S(2)}) copy-start(bf16[128]{0:T(256)(128)(2,1)} %param.31) | copy-start | bytes 772
  1546.9 549.3 %all-gather.34.cloned.1.call-start = ((), (), s32[]{:S(2)}) async-start(), calls=%async_computation.20 | async-start | bytes 3932160 | tf_op jit(solution)/shard_map/all_gather | solution.py:14
  1883.1 2.8 copy-start.1
  1886.4 1.6 copy-start.10
  1889.5 1.6 copy-start.12
  (23 other events, 30.9 us)
Sparse Core Ops, SparseCore 0:
  10.2 101.8 all-gather.15
  122.9 36.3 all-gather.17
  161.5 49.2 all-gather.19
  212.8 123.4 all-gather.21
  338.3 123.1 all-gather.25
  463.4 123.1 all-gather.27
  588.7 47.6 all-gather.29
  640.0 86.3 reduce-scatter.15
  730.7 282.4 reduce-scatter.17
  1016.8 281.8 reduce-scatter.19
  1302.2 134.2 all-reduce.9
  1438.8 99.2 all-gather.31
  1542.0 205.5 reduce-scatter.13
  1749.8 124.7 all-gather.23
  1878.2 60.1 reduce-scatter.25
  1941.6 60.9 reduce-scatter.23
  2006.1 60.9 reduce-scatter.21
  2068.6 27.5 all-gather.33
